TPU v7x, 32 devices: a whole 2x2x4 slice. The times are simulated.
32 devices in a mesh: band: 16 (over z, x, core), ga: 2 (over y).
Axes of the slice: x: 2, y: 2, z: 4, core: 2. Of those that a mesh axis runs over, the one named last changes fastest.
Arguments:
- psi: float32 [8192, 8192], P('ga', 'band'), may hold values from -6 to 6
- tiles: float32 [16, 3, 512, 512], P('band', None, 'ga'), may hold values from -0.1875 to 0.1875
- half_width: int32 [1], replicated, may hold values from 384 to 512
Outputs:
- rotated: float32 [8192, 8192], P('ga', 'band')
All inputs are finite; a program needn't handle non-finite values.
Results may differ from a plain program's by a relative error of at most 0.0001.
Values sent between devices are 32-bit elements; how exact they have to be, the bound alone decides.
A program may use at most 128 MiB of HBM per device.

v0:
```python
import jax
import jax.numpy as jnp
from jax import lax
from jax.sharding import PartitionSpec as P


def shifted(block, axis, distance):
    devices = range(lax.axis_size(axis))
    route = [(i - distance, i) for i in devices if i - distance in devices]
    return lax.ppermute(block, axis, route)


def band_mask(span, width, half_width):
    reach = (span - 1) // 2
    index = jnp.arange(width)
    shifts = (jnp.arange(span) - reach) * width
    offsets = shifts[:, None, None] + index[None, :, None] - index[None, None, :]
    return (jnp.abs(offsets) <= half_width[0]).astype(jnp.float32)


def on_device(psi, tiles, half_width):
    whole = lax.all_gather(tiles, "ga", axis=2, tiled=True)
    span, width = (whole.shape[1], whole.shape[2])
    reach = (span - 1) // 2
    masked = whole[0] * band_mask(span, width, half_width)
    neighbours = {reach: psi}
    for k in range(span):
        if k != reach:
            neighbours[k] = shifted(psi, "band", reach - k)
    stacked = jnp.concatenate([neighbours[k] for k in range(span)], axis=1)
    return jnp.dot(
        stacked,
        masked.reshape(span * width, width),
        precision=lax.Precision.HIGHEST,
        preferred_element_type=jnp.float32,
    )


def solution(mesh):
    return jax.shard_map(
        on_device,
        mesh=mesh,
        in_specs=(P("ga", "band"), P("band", None, "ga", None), P()),
        out_specs=P("ga", "band"),
        check_vma=False,
    )
```

profile of v0, /device:TPU:1, one launch (start us, length us, event | category | flops | bytes accessed | tf_op | source)
XLA Modules:
  0.0 242.4 jit_solution(12512618287407158787)
XLA Ops:
  6.5 0.0 all-gather.2.cloned.1.call-start
  6.5 4.5 %collective-permute-start = (f32[4096,512]{1,0:T(8,128)}, f32[4096,512]{1,0:T(8,128)}, u32[]{:S(2)}, u32[]{:S(2)}) collective-permute-start(f32[4096,512]{1,0:T(8,128)} %param.3), channel_id=1, source_target_pairs={{0,2},{2,4},{4,6},{6,8},{8,10},{10,12},{12,14},{14,16},{16,18},{18... | collective-permute-start | bytes 25165832 | tf_op jit(solution)/shard_map/ppermute | solution.py:10
  11.0 3.0 %collective-permute-start.1 = (f32[4096,512]{1,0:T(8,128)}, f32[4096,512]{1,0:T(8,128)}, u32[]{:S(2)}, u32[]{:S(2)}) collective-permute-start(f32[4096,512]{1,0:T(8,128)} %param.3), channel_id=1, source_target_pairs={{2,0},{4,2},{6,4},{8,6},{10,8},{12,10},{14,12},{16,14},{18,16},{20... | collective-permute-start | bytes 25165832 | tf_op jit(solution)/shard_map/ppermute | solution.py:10
  14.1 0.0 all-gather.2.cloned.1.call-update
  14.8 0.1 iota_add_fusion
  14.8 45.9 %all-gather.2.cloned.1.call-done = f32[1,3,512,512]{3,2,1,0:T(8,128)} async-done(((f32[1,3,256,512]{3,2,1,0:T(8,128)}), f32[1,3,512,512]{3,2,1,0:T(8,128)}) %all-gather.2.cloned.1.call-update) | async-done | bytes 3145744 | tf_op jit(solution)/shard_map/all_gather | solution.py:22
  60.7 2.6 %bitcast_select_fusion = f32[1536,512]{1,0:T(8,128)S(1)} fusion(f32[1,3,512,512]{3,2,1,0:T(8,128)} %all-gather.2.cloned.1.call-done, s32[]{:T(128)} %bitcast.4, s32[1536]{0:T(1024)S(1)} %add.29), kind=kLoop, calls=%fused_computation.6 | loop fusion | flops 3145728 | bytes 6297604 | tf_op jit(solution)/shard_map/mul | solution.py:25
  63.3 128.3 %collective-permute-done = f32[4096,512]{1,0:T(8,128)} collective-permute-done((f32[4096,512]{1,0:T(8,128)}, f32[4096,512]{1,0:T(8,128)}, u32[]{:S(2)}, u32[]{:S(2)}) %collective-permute-start) | collective-permute-done | bytes 8388640 | tf_op jit(solution)/shard_map/ppermute | solution.py:10
  191.6 0.0 collective-permute-done.1
  191.6 44.0 %fusion = f32[4096,512]{1,0:T(8,128)} fusion(f32[1536,512]{1,0:T(8,128)S(1)} %bitcast_select_fusion, f32[4096,512]{1,0:T(8,128)} %collective-permute-done.1, f32[4096,512]{1,0:T(8,128)} %param.3, f32[4096,512]{1,0:T(8,128)} %collective-permute-done), kind=kOutput, calls=%fused_computation | convolution fusion | flops 38667288576 | bytes 36700160 | tf_op jit(solution)/shard_map/dot_general | solution.py:31
  (2 shorter events, 0.0 us)
Async XLA Ops:
  6.5 54.2 %all-gather.2.cloned.1.call-start = ((), (), s32[]{:S(2)}) async-start(), calls=%async_computation | async-start | bytes 4718592 | tf_op jit(solution)/shard_map/all_gather | solution.py:22
  6.5 185.1 %collective-permute-start = (f32[4096,512]{1,0:T(8,128)}, f32[4096,512]{1,0:T(8,128)}, u32[]{:S(2)}, u32[]{:S(2)}) collective-permute-start(f32[4096,512]{1,0:T(8,128)} %param.3), channel_id=1, source_target_pairs={{0,2},{2,4},{4,6},{6,8},{8,10},{10,12},{12,14},{14,16},{16,18},{18... | collective-permute-start | bytes 25165832 | tf_op jit(solution)/shard_map/ppermute | solution.py:10
  11.0 180.6 %collective-permute-start.1 = (f32[4096,512]{1,0:T(8,128)}, f32[4096,512]{1,0:T(8,128)}, u32[]{:S(2)}, u32[]{:S(2)}) collective-permute-start(f32[4096,512]{1,0:T(8,128)} %param.3), channel_id=1, source_target_pairs={{2,0},{4,2},{6,4},{8,6},{10,8},{12,10},{14,12},{16,14},{18,16},{20... | collective-permute-start | bytes 25165832 | tf_op jit(solution)/shard_map/ppermute | solution.py:10
Sparse Core Ops, SparseCore 0:
  14.2 46.4 all-gather.1
where the time goes:
time: 243 us; the launch traced here: 242 us
  waiting for transfers between devices  174 us (72%)
  matrix products  44 us (18%)
  between operations  14.1 us (6%)
  starting transfers between devices  7.53 us (3%)
  other arithmetic  2.64 us (1%)
    ppermute x2, waiting for transfers between devices, shifted(): return lax.ppermute(block, axis, route)  128 us
    all_gather x1, waiting for transfers between devices, on_device(): whole = lax.all_gather(tiles, 'ga', axis=2, tiled=True)  45.9 us
    dot_general x1, matrix products, on_device(): jnp.dot(stacked, masked.reshape(span * width, width), precision=lax.Preci...  44 us
    ppermute x2, starting transfers between devices, shifted(): return lax.ppermute(block, axis, route)  7.52 us
  transfers between devices with their start and end apart: 3, of which 2 were waited for; matrix products, arithmetic and copies ran while one was open for 1% of the time, Pallas kernels for 0%

commit v1 on v0

v1 whole, which is shorter than its diff:
```python
import functools

import jax
import jax.numpy as jnp
from jax import lax
from jax.experimental import pallas as pl
from jax.experimental.pallas import tpu as pltpu
from jax.sharding import PartitionSpec as P

MESH = pl.DeviceIdType.MESH
CHUNKS = 16


def split(x):
    high = x.astype(jnp.bfloat16)
    return high, (x - high.astype(jnp.float32)).astype(jnp.bfloat16)


def product(x, high, low):
    x_high, x_low = split(x)
    dot = functools.partial(jnp.dot, preferred_element_type=jnp.float32)
    return dot(x_high, high) + (dot(x_high, low) + dot(x_low, high))


def kernel(n, n_ga, plane, hw_ref, psi, tiles, out, own, near, relay, raw, high, low,
           own_sem, tile_send, tile_recv, send, recv, relay_send, relay_recv, forward_send):
    me = lax.axis_index("band")
    ga = lax.axis_index("ga")
    rows, width = psi.shape
    span, part = tiles.shape[1], tiles.shape[2]
    reach = (span - 1) // 2
    chunk = rows // CHUNKS
    planes = n // plane
    relays = plane >= 4 and planes > 1
    moves = [s * m for m in range(1, reach + 1) for s in (1, -1)]
    at, last = lax.rem(me, plane), lax.div(me, plane)

    peers = []
    for move in moves:
        there = me + move
        peers.append(((there >= 0) & (there < n), there))
        back = me - move
        peers.append(((back >= 0) & (back < n), back))
    up_src = (at == plane - 1) & (last < planes - 1)
    up_mid = (at == 0) & (last < planes - 1)
    up_dst = (at == 0) & (last > 0)
    down_src = (at == 0) & (last > 0)
    down_mid = (at == plane - 2) & (last > 0)
    down_dst = (at == plane - 1) & (last < planes - 1)
    up_mid_of_src = me - (plane - 1)
    down_mid_of_src = me + (plane - 2)
    if relays:
        peers += [
            (up_src, me - (plane - 1)), (up_mid, me + (plane - 1)),
            (up_mid, me + plane), (up_dst, me - plane),
            (down_src, me + (plane - 2)), (down_mid, me - (plane - 2)),
            (down_mid, me - (plane - 1)), (down_dst, me + (plane - 1)),
        ]
    barrier = pltpu.get_barrier_semaphore()
    count = jnp.int32(n_ga - 1)
    for step in range(1, n_ga):
        pl.semaphore_signal(barrier, inc=1, device_id=(me, lax.rem(ga + step, n_ga)), device_id_type=MESH)
    for cond, peer in peers:
        @pl.when(cond)
        def _(peer=peer):
            pl.semaphore_signal(barrier, inc=1, device_id=(peer, ga), device_id_type=MESH)
        count = count + cond.astype(jnp.int32)
    pl.semaphore_wait(barrier, count)

    def block(c):
        return pl.ds(pl.multiple_of(c * chunk, chunk), chunk)

    def direct_copy(slot, move, c):
        return pltpu.make_async_remote_copy(
            psi.at[block(c)], near.at[slot, block(c)], send.at[slot, c], recv.at[slot, c],
            device_id=(me + move, ga), device_id_type=MESH)

    def relay_copy(slot, mid, c):
        return pltpu.make_async_remote_copy(
            psi.at[block(c)], relay.at[block(c)], send.at[slot, c], relay_recv.at[c],
            device_id=(mid, ga), device_id_type=MESH)

    def forward_copy(slot, to, c):
        return pltpu.make_async_remote_copy(
            relay.at[block(c)], near.at[slot, block(c)], forward_send.at[c], recv.at[slot, c],
            device_id=(to, ga), device_id_type=MESH)

    def goes_up(p, c):
        return lax.rem(c, planes) < planes - 1 - p

    def goes_down(p, c):
        return lax.rem(c, planes) < p

    def tile_copy(step):
        peer = lax.rem(ga + step, n_ga)
        return pltpu.make_async_remote_copy(
            tiles.at[0], raw.at[:, pl.ds(pl.multiple_of(ga * part, part), part), :],
            tile_send.at[step - 1], tile_recv.at[step - 1],
            device_id=(me, peer), device_id_type=MESH)

    for step in range(1, n_ga):
        tile_copy(step).start()

    def start(c, carry):
        for slot, move in enumerate(moves):
            there = me + move
            valid = (there >= 0) & (there < n)
            if relays and abs(move) == 1:
                src, mid = (up_src, up_mid_of_src) if move == 1 else (down_src, down_mid_of_src)
                via = src & (goes_up(last, c) if move == 1 else goes_down(last, c))

                @pl.when(via)
                def _():
                    relay_copy(slot, mid, c).start()
                valid = valid & jnp.logical_not(via)

            @pl.when(valid)
            def _():
                direct_copy(slot, move, c).start()
        return carry
    lax.fori_loop(0, CHUNKS, start, 0)

    own_tiles = pltpu.make_async_copy(
        tiles.at[0], raw.at[:, pl.ds(pl.multiple_of(ga * part, part), part), :], own_sem.at[1])
    own_tiles.start()
    own_psi = pltpu.make_async_copy(psi, own, own_sem.at[0])
    own_psi.start()
    own_tiles.wait()
    for step in range(1, n_ga):
        tile_copy(step).wait_recv()
    half = hw_ref[0]
    piece = min(width, 128)
    for k in range(span):
        for r in range(0, width, piece):
            row = lax.broadcasted_iota(jnp.int32, (piece, width), 0) + (r + (k - reach) * width)
            col = lax.broadcasted_iota(jnp.int32, (piece, width), 1)
            u = jnp.where(jnp.abs(row - col) <= half, raw[k, r:r + piece, :], 0.0)
            u_high, u_low = split(u)
            high[k, r:r + piece, :] = u_high
            low[k, r:r + piece, :] = u_low
    own_psi.wait()

    def centre(c, carry):
        out[block(c), :] = product(own[block(c), :], high[reach], low[reach])
        return carry
    lax.fori_loop(0, CHUNKS, centre, 0)

    def step(c, carry):
        if relays:
            @pl.when(up_mid & goes_up(last, c))
            def _():
                relay_copy(0, me, c).wait_recv()
                forward_copy(0, me + plane, c).start()

            @pl.when(down_mid & goes_down(last, c))
            def _():
                relay_copy(1, me, c).wait_recv()
                forward_copy(1, me - (plane - 1), c).start()
        for slot, move in enumerate(moves):
            back = me - move

            @pl.when((back >= 0) & (back < n))
            def _():
                direct_copy(slot, move, c).wait_recv()
                k = reach - move
                out[block(c), :] += product(near[slot, block(c), :], high[k], low[k])
        return carry
    lax.fori_loop(0, CHUNKS, step, 0)

    def finish(c, carry):
        for slot, move in enumerate(moves):
            there = me + move

            @pl.when((there >= 0) & (there < n))
            def _():
                direct_copy(slot, move, c).wait_send()
        if relays:
            @pl.when((up_mid & goes_up(last, c)) | (down_mid & goes_down(last, c)))
            def _():
                forward_copy(0, me, c).wait_send()
        return carry
    lax.fori_loop(0, CHUNKS, finish, 0)
    for step_ in range(1, n_ga):
        tile_copy(step_).wait_send()


def plane_size(mesh):
    axis = mesh.axis_names.index("band")
    line = mesh.devices.take(0, axis=1 - axis)
    coords = [getattr(d, "coords", None) for d in line]
    if coords[0] is None:
        return len(coords)
    return sum(c[2] == coords[0][2] for c in coords)


def solution(mesh):
    n, n_ga = mesh.shape["band"], mesh.shape["ga"]
    plane = plane_size(mesh)

    def on_device(psi, tiles, half_width):
        rows, width = psi.shape
        span = tiles.shape[1]
        f32, bf16 = jnp.float32, jnp.bfloat16
        dma = pltpu.SemaphoreType.DMA
        sides = span - 1
        return pl.pallas_call(
            functools.partial(kernel, n, n_ga, plane),
            out_shape=jax.ShapeDtypeStruct((rows, width), f32),
            in_specs=[
                pl.BlockSpec(memory_space=pltpu.SMEM),
                pl.BlockSpec(memory_space=pl.ANY),
                pl.BlockSpec(memory_space=pl.ANY),
            ],
            out_specs=pl.BlockSpec(memory_space=pltpu.VMEM),
            scratch_shapes=[
                pltpu.VMEM((rows, width), f32),
                pltpu.VMEM((sides, rows, width), f32),
                pltpu.VMEM((rows, width), f32),
                pltpu.VMEM((span, width, width), f32),
                pltpu.VMEM((span, width, width), bf16),
                pltpu.VMEM((span, width, width), bf16),
                dma((2,)),
                dma((n_ga - 1,)),
                dma((n_ga - 1,)),
                dma((sides, CHUNKS)),
                dma((sides, CHUNKS)),
                dma((CHUNKS,)),
                dma((CHUNKS,)),
                dma((CHUNKS,)),
            ],
            compiler_params=pltpu.CompilerParams(
                collective_id=0, has_side_effects=True, vmem_limit_bytes=60 * 2**20),
            name="rotate",
        )(half_width, psi, tiles)

    return jax.shard_map(
        on_device,
        mesh=mesh,
        in_specs=(P("ga", "band"), P("band", None, "ga", None), P()),
        out_specs=P("ga", "band"),
        check_vma=False,
    )
```

time: 243 us -> 176 us (0.72)
  waiting for transfers between devices: 174 us -> 0 us
  Pallas kernels: 0 us -> 168 us
  matrix products: 44 us -> 0 us
  between operations: 14.1 us -> 0.66 us
  local copies, waits for them, and re-layouts: 0.01 us -> 7.76 us
  starting transfers between devices: 7.53 us -> 0 us
  other arithmetic: 2.64 us -> 0 us
    pallas_call x0 -> x1, Pallas kernels: none -> 168 us  [on_device(): pl.pallas_call(functools.partial(kernel, n, n_ga, plane), out_shape=jax.S...]
    ppermute x2 -> x0, waiting for transfers between devices: 128 us -> none  [shifted(): return lax.ppermute(block, axis, route)]
    all_gather x1 -> x0, waiting for transfers between devices: 45.9 us -> none  [on_device(): whole = lax.all_gather(tiles, 'ga', axis=2, tiled=True)]
    dot_general x1 -> x0, matrix products: 44 us -> none  [on_device(): jnp.dot(stacked, masked.reshape(span * width, width), precision=lax.Preci...]
    unnamed x0 -> x1, local copies, waits for them, and re-layouts: none -> 7.76 us
    ppermute x2 -> x0, starting transfers between devices: 7.52 us -> none  [shifted(): return lax.ppermute(block, axis, route)]
    mul x2 -> x0, other arithmetic: 2.57 us -> none  [the longest x1 2.56 us: on_device(): masked = whole[0] * band_mask(span, width, half_width)]
  transfers between devices with their start and end apart: 3 -> 0, of which waited for: 2 -> 0; matrix products, arithmetic and copies ran while one was open for 1% -> 0% of each run, Pallas kernels for 0% -> 0%
where the time goes in v1:
time: 176 us
  Pallas kernels  168 us (95%)
  local copies, waits for them, and re-layouts  7.76 us (4%)
    pallas_call x1, Pallas kernels, on_device(): pl.pallas_call(functools.partial(kernel, n, n_ga, plane), out_shape=jax.S...  168 us
    unnamed x1, local copies, waits for them, and re-layouts  7.76 us

profile of v1, /device:TPU:1, one launch (start us, length us, event | category | flops | bytes accessed | tf_op | source)
XLA Modules:
  0.0 176.0 jit_solution(4375870739916706364)
XLA Ops:
  0.7 167.6 %rotate.1 = f32[4096,512]{1,0:T(8,128)} custom-call(s32[1]{0:T(128)S(6)} %copy.5.hw_ref, f32[4096,512]{1,0:T(8,128)} %psi.1, f32[1,3,256,512]{3,2,1,0:T(8,128)} %tiles.1), custom_call_target="tpu_custom_call" | custom-call | tf_op jit(solution)/shard_map/rotate/pallas_call | solution.py:206
  168.2 7.8 %copy.6 = f32[4096,512]{1,0:T(8,128)} copy(f32[4096,512]{1,0:T(8,128)} %rotate.1) | data formatting | bytes 16777216
